TPU v7x, 512 devices: a whole 4x8x8 slice. The times are simulated.
512 devices in a mesh: req: 64 (over x, y_hi, z), tp: 8 (over y_lo, core).
Axes of the slice: x: 4, y: 8 (y_hi: 2, y_lo: 4; y = y_hi * 4 + y_lo), z: 8, core: 2. Of those that a mesh axis runs over, the one named last changes fastest.
Arguments:
- states: bfloat16 [64, 256, 1536], P('req', 'tp'), may hold values from -7 to 7
- gain_attn: bfloat16 [1536], replicated, may hold values from 0.25 to 1.75
- gain_moe: bfloat16 [1536], replicated, may hold values from 0.25 to 1.75
- w_query: bfloat16 [1536, 1536], P(None, 'tp'), may hold values from -4 to 4
- w_keyval: bfloat16 [1536, 1024], P(None, 'tp'), may hold values from -4 to 4
- w_out: bfloat16 [1536, 1536], P('tp'), may hold values from -0.875 to 0.875
- prefix_cache: bfloat16 [64, 128, 1024], P('req', None, 'tp'), may hold values from -6 to 6
- w_gate_up: bfloat16 [64, 1536, 512], P('req'), may hold values from -0.15625 to 0.15625
- w_down: bfloat16 [64, 256, 1536], P('req'), may hold values from -0.25 to 0.25
- routes: int32 [64, 256, 8], P('req', 'tp'), may hold values from 0 to 31, all different within a row; in each aligned block of 32 rows (0 to 31, 32 to 63, ..., all dimensions but the last counted through in order) at most 10 rows name the same one
- gates: float32 [64, 256, 8], P('req', 'tp'), may hold values from 0.05 to 0.3
- lengths: int32 [64], replicated, may hold values from 1 to 256, 14336 in all
- group_of: int32 [64], replicated, may hold values from 0 to 15
- owners: int32 [64], replicated, may hold values from 0 to 63, each once
Outputs:
- layer_out: bfloat16 [64, 256, 1536], P('req', 'tp')
Inputs may be any that keep to these rules, and one draw needn't show every extreme that they name: `routes`: in each aligned block of 32 rows (all leading dimensions taken together, in order) no expert is named by more than 10 rows, a bound that some block reaches. `owners`: each index of req appears once.
All inputs are finite; a program needn't handle non-finite values.
Results may differ from a plain program's by a relative error of at most 0.02.
Values may be sent and summed in bfloat16 or wider, within the bound.
No kernel may reach another device: no remote copies, remote signals or barrier semaphores. Data moves between devices by JAX's collectives and lax.ppermute only.
A program may use at most 64 MiB of HBM per device.

v0:
```python
import math
import jax
import jax.numpy as jnp
from jax import lax
from jax.sharding import PartitionSpec as P

D = 1536
HD = 64
EXPERTS = 32
TOPK = 8
PIECES = 4


def rms_scale(values, gain):
    spread = lax.rsqrt(jnp.mean(values * values, axis=-1, keepdims=True) + 1e-05)
    return values * spread * gain.astype(jnp.float32)


def apply_rotary(tensor, offset):
    count = tensor.shape[0]
    width = tensor.shape[-1] // 2
    place = offset + jnp.arange(count, dtype=jnp.float32)
    freq = jnp.exp(
        jnp.arange(width, dtype=jnp.float32) * (-2.0 * math.log(10000.0) / tensor.shape[-1])
    )
    angle = place[:, None] * freq[None, :]
    cosine = jnp.cos(angle)[:, None, :]
    sine = jnp.sin(angle)[:, None, :]
    first = tensor[..., :width]
    second = tensor[..., width:]
    return jnp.concatenate(
        [first * cosine - second * sine, second * cosine + first * sine], axis=-1
    )


def softmax_step(state, grouped, keys, values, keep):
    top, total, accum = state
    scores = jnp.einsum("hqd,khd->hqk", grouped, keys, preferred_element_type=jnp.float32) * (
        1.0 / math.sqrt(HD)
    )
    scores = jnp.where(keep, scores, -1e30)
    new_top = jnp.maximum(top, jnp.max(scores, axis=-1))
    weights = jnp.where(keep, jnp.exp(scores - new_top[..., None]), 0.0)
    fade = jnp.exp(top - new_top)
    total = total * fade + jnp.sum(weights, axis=-1)
    accum = accum * fade[..., None] + jnp.einsum(
        "hqk,khd->hqd", weights.astype(jnp.bfloat16), values, preferred_element_type=jnp.float32
    )
    return (new_top, total, accum)


def on_device(
    states,
    gain_attn,
    gain_moe,
    w_query,
    w_keyval,
    w_out,
    prefix_cache,
    w_gate_up,
    w_down,
    routes,
    gates,
    lengths,
    group_of,
    owners,
):
    devices_req = lax.axis_size("req")
    devices_tp = lax.axis_size("tp")
    mine = lax.axis_index("req")
    column = lax.axis_index("tp")
    local_rows = states.shape[1]
    full_rows = local_rows * devices_tp
    segment = prefix_cache.shape[1]
    plen = PIECES * segment
    length = lengths[mine]
    group = group_of[mine]
    resid_in = states[0].astype(jnp.float32)
    normed = rms_scale(resid_in, gain_attn).astype(jnp.bfloat16)
    gathered = lax.all_gather(normed, "tp", axis=0, tiled=True)
    q_heads = w_query.shape[1] // HD
    kv_heads = w_keyval.shape[1] // (2 * HD)
    per_kv = q_heads // kv_heads
    query_rows = jnp.dot(gathered, w_query, preferred_element_type=jnp.float32).reshape(
        full_rows, q_heads, HD
    )
    query_rows = apply_rotary(query_rows, float(plen)).astype(jnp.bfloat16)
    keyvals = jnp.dot(gathered, w_keyval, preferred_element_type=jnp.float32).reshape(
        full_rows, kv_heads, 2, HD
    )
    keys = apply_rotary(keyvals[:, :, 0], float(plen)).astype(jnp.bfloat16)
    values = keyvals[:, :, 1].astype(jnp.bfloat16)
    grouped = (
        query_rows.reshape(full_rows, kv_heads, per_kv, HD)
        .transpose(1, 2, 0, 3)
        .reshape(kv_heads, per_kv * full_rows, HD)
    )
    holder = jnp.arange(devices_req, dtype=jnp.int32)
    match = owners[None, :] == holder[:, None]
    piece_group = jnp.sum(jnp.where(match, holder[None, :], 0), axis=1) // PIECES
    start_state = (
        jnp.full((kv_heads, per_kv * full_rows), -1e30, jnp.float32),
        jnp.zeros((kv_heads, per_kv * full_rows), jnp.float32),
        jnp.zeros((kv_heads, per_kv * full_rows, HD), jnp.float32),
    )
    owned = piece_group == group

    def one_piece(state, inputs):
        block, flag = inputs
        block = block.reshape(segment, kv_heads, 2, HD)

        def update(inner_state):
            keep = jnp.ones((1, 1, segment), jnp.bool_)
            return softmax_step(inner_state, grouped, block[:, :, 0], block[:, :, 1], keep)

        return (lax.cond(flag, update, lambda inner_state: inner_state, state), None)

    result, unused = lax.scan(
        one_piece, start_state, (lax.all_gather(prefix_cache, "req", axis=0, tiled=True), owned)
    )
    state = result
    key_at = jnp.arange(full_rows)
    query_position = jnp.arange(per_kv * full_rows) % full_rows
    keep = (key_at[None, :] <= query_position[:, None]) & (key_at[None, :] < length)
    top, total, accum = softmax_step(state, grouped, keys, values, keep[None])
    mixed = (
        (accum / total[..., None]).reshape(kv_heads, per_kv, full_rows, HD).transpose(2, 0, 1, 3)
    )
    mixed = mixed.reshape(full_rows, q_heads * HD).astype(jnp.bfloat16)
    attended = lax.psum_scatter(
        jnp.dot(mixed, w_out, preferred_element_type=jnp.float32).astype(jnp.bfloat16),
        "tp",
        scatter_dimension=0,
        tiled=True,
    ).astype(jnp.float32)
    residual = resid_in + attended
    normed_moe = rms_scale(residual, gain_moe).astype(jnp.bfloat16)
    chosen = routes[0].reshape(-1)
    onehot = (chosen[:, None] == jnp.arange(EXPERTS, dtype=jnp.int32)[None, :]).astype(jnp.int32)
    slot_in = jnp.sum(jnp.cumsum(onehot, axis=0) * onehot, axis=1) - 1
    source = jnp.arange(chosen.shape[0], dtype=jnp.int32) // TOPK
    capacity = max(2, 5 * full_rows // (16 * devices_tp))
    outbound = (
        jnp.zeros((EXPERTS, capacity, D), jnp.bfloat16).at[chosen, slot_in].set(normed_moe[source])
    )
    slot_dev = 2 * EXPERTS // devices_req
    outgoing = jnp.repeat(outbound, 2, axis=0).reshape(devices_req, slot_dev, capacity, D)
    half_units = w_down.shape[1]
    pair = jnp.einsum(
        "nskd,sdf->nskf",
        lax.all_to_all(outgoing, "req", split_axis=0, concat_axis=0, tiled=True),
        w_gate_up,
        preferred_element_type=jnp.float32,
    )
    inner = (jax.nn.silu(pair[..., :half_units]) * pair[..., half_units:]).astype(jnp.bfloat16)
    produced = jnp.einsum(
        "nskf,sfd->nskd", inner, w_down, preferred_element_type=jnp.float32
    ).astype(jnp.bfloat16)
    returned = lax.all_to_all(produced, "req", split_axis=0, concat_axis=0, tiled=True)
    summed = jnp.sum(returned.reshape(EXPERTS, 2, capacity, D).astype(jnp.float32), axis=1).reshape(
        EXPERTS * capacity, D
    )
    selected_experts = summed[chosen * capacity + slot_in].reshape(local_rows, TOPK, D)
    expert_blend = jnp.einsum(
        "hv,hva->ha", gates[0], selected_experts, precision=lax.Precision.HIGHEST
    )
    row_at = column * local_rows + jnp.arange(local_rows)
    final = jnp.where((row_at < length)[:, None], residual + expert_blend, 0.0).astype(jnp.bfloat16)
    return final[None]


def solution(mesh):
    placed = (
        P("req", "tp", None),
        P(),
        P(),
        P(None, "tp"),
        P(None, "tp"),
        P("tp", None),
        P("req", None, "tp"),
        P("req", None, None),
        P("req", None, None),
        P("req", "tp", None),
        P("req", "tp", None),
        P(),
        P(),
        P(),
    )
    return jax.shard_map(
        on_device, mesh=mesh, in_specs=placed, out_specs=P("req", "tp", None), check_vma=False
    )
```

profile of v0, /device:TPU:1, one launch (start us, length us, event | category | flops | bytes accessed | tf_op | source)
XLA Modules:
  0.0 505.0 jit_solution(2194904492589218272)
XLA Ops:
  10.3 22.7 %all_gather.7 = bf16[256,1536]{1,0:T(8,128)(2,1)S(1)} all-gather(bf16[32,1536]{1,0:T(8,128)(2,1)S(1)} %fusion.37), channel_id=1, replica_groups=mesh['req'=64,'tp'=8] {'tp'}, dimensions={0}, use_global_device_ids=true | all-gather | bytes 884736 | tf_op jit(solution)/shard_map/all_gather | solution.py:80
  33.0 1.5 fusion.79
  39.0 1.3 fusion.78
  40.3 106.8 %all-gather.2.cloned.1.call-done = bf16[64,128,128]{2,1,0:T(8,128)(2,1)} async-done(((bf16[1,128,128]{2,1,0:T(8,128)(2,1)}), bf16[64,128,128]{2,1,0:T(8,128)(2,1)}) %all-gather.2.cloned.1.call-update) | async-done | bytes 2097168 | tf_op jit(solution)/shard_map/all_gather | solution.py:119
  147.1 4.1 copy.42
  151.3 87.6 %while.14 = (s32[]{:T(128)}, f32[1,768]{1,0:T(1,128)S(1)}, f32[1,768]{1,0:T(1,128)S(1)}, f32[1,768,64]{1,2,0:T(8,128)S(1)}, pred[64]{0:T(512)(128)(4,1)S(1)}, /*...) while((s32[]{:T(128)}, f32[1,768]{1,0:T(1,128)S(1)}, f32[1,768]{1,0:T(1,128)S(1)}, ...), condition=%wide.region_7.8_spmd, body=%wide.region_2.7_spmd.sunk | while | flops 25856260 | bytes 1922252 | solution.py:118
  158.9 1.4 conditional.2
  191.1 1.4 conditional.2
  198.9 1.4 conditional.2
  215.7 1.4 conditional.2
  241.3 1.3 convolution_convert_fusion.1
  243.9 35.9 %reduce-scatter.2.cloned.1.call-done = bf16[32,1536]{1,0:T(8,128)(2,1)} async-done(((bf16[256,1536]{1,0:T(8,128)(2,1)}), bf16[32,1536]{1,0:T(8,128)(2,1)}) %reduce-scatter.2.cloned.1.call-update) | async-done | bytes 98320 | tf_op jit(solution)/shard_map/reduce_scatter | solution.py:130
  281.9 1.3 gather_fusion
  283.2 19.5 %scatter_fusion = bf16[32,10,1536]{2,0,1:T(8,128)(2,1)S(1)} fusion(bf16[32,10,1536]{2,0,1:T(8,128)(2,1)S(1)} %broadcast_in_dim.99, s32[256]{0:T(256)S(1)} %bitcast.143, bf16[256,1536]{1,0:T(8,128)(2,1)S(1)} %gather_fusion), kind=kCustom, calls=%fused_computation.2 | custom fusion | bytes 2361344 | tf_op jit(solution)/shard_map/scatter | solution.py:144
  303.7 89.7 %all_to_all.10 = bf16[64,1,10,1536]{3,2,1,0:T(8,128)(2,1)S(1)} all-to-all(bf16[64,1,10,1536]{3,2,1,0:T(8,128)(2,1)S(1)} %bitcast.144), channel_id=1, replica_groups=mesh['req'=64,'tp'=8] {'req'}, dimensions={0} | all-to-all | bytes 3932160 | tf_op jit(solution)/shard_map/all_to_all | solution.py:151
  393.3 1.3 fusion.14
  395.3 2.9 copy.50
  398.2 9.3 %all-to-all-start.1 = ((bf16[64,1,10,1536]{3,2,1,0:T(8,128)(2,1)}), bf16[64,1,10,1536]{3,2,1,0:T(8,128)(2,1)}, u32[]{:S(2)}, u32[]{:S(2)}) async-start(bf16[64,1,10,1536]{3,2,1,0:T(8,128)(2,1)} %copy.50), calls=%async_computation.2 | async-start | bytes 6291456 | tf_op jit(solution)/shard_map/all_to_all | solution.py:159
  409.4 75.0 %all-to-all-done.1 = bf16[64,1,10,1536]{3,2,1,0:T(8,128)(2,1)} async-done(((bf16[64,1,10,1536]{3,2,1,0:T(8,128)(2,1)}), bf16[64,1,10,1536]{3,2,1,0:T(8,128)(2,1)}, u32[]{:S(2)}, u32[]{:S(2)}) %all-to-all-start.1) | async-done | bytes 1966112 | tf_op jit(solution)/shard_map/all_to_all | solution.py:159
  484.4 4.8 convert_reduce_fusion
  489.2 2.0 reshape.446
  491.2 2.5 gather_fusion.1
  493.7 2.8 fusion.11
  496.5 1.7 fusion.44
  (233 shorter events, 61.6 us)
Async XLA Ops:
  6.5 386.8 %copy-start = (bf16[1,1536,512]{2,1,0:T(8,128)(2,1)S(1)}, bf16[1,1536,512]{2,1,0:T(8,128)(2,1)}, u32[]{:S(2)}) copy-start(bf16[1,1536,512]{2,1,0:T(8,128)(2,1)} %param.25) | copy-start | bytes 4718596
  6.5 140.6 %all-gather.2.cloned.1.call-start = ((), (), s32[]{:S(2)}) async-start(), calls=%async_computation.3 | async-start | bytes 2129920 | tf_op jit(solution)/shard_map/all_gather | solution.py:119
  7.3 272.6 %reduce-scatter.2.cloned.1.call-start = ((), (), s32[]{:S(2)}) async-start(), calls=%async_computation.4 | async-start | bytes 884736 | tf_op jit(solution)/shard_map/reduce_scatter | solution.py:130
  10.2 25.3 %copy-start.8 = (s32[64]{0:T(128)S(1)}, s32[64]{0:T(128)}, u32[]{:S(2)}) copy-start(s32[64]{0:T(128)} %param.29) | copy-start | bytes 772
  10.3 26.0 %copy-start.9 = (s32[64]{0:T(128)S(1)}, s32[64]{0:T(128)}, u32[]{:S(2)}) copy-start(s32[64]{0:T(128)} %param.30) | copy-start | bytes 772
  10.3 27.3 %copy-start.10 = (s32[64]{0:T(128)S(1)}, s32[64]{0:T(128)}, u32[]{:S(2)}) copy-start(s32[64]{0:T(128)} %param.31) | copy-start | bytes 772
  10.3 28.1 %copy-start.3 = (bf16[1536,128]{1,0:T(8,128)(2,1)S(1)}, bf16[1536,128]{1,0:T(8,128)(2,1)}, u32[]{:S(2)}) copy-start(bf16[1536,128]{1,0:T(8,128)(2,1)} %param.22) | copy-start | bytes 1179652
  238.9 2.3 copy-start.2
  239.2 3.3 copy-start.4
  239.2 3.7 copy-start.5
  240.2 39.6 %copy-start.1 = (bf16[1,32,1536]{2,1,0:T(8,128)(2,1)S(1)}, bf16[1,32,1536]{2,1,0:T(8,128)(2,1)}, u32[]{:S(2)}) copy-start(bf16[1,32,1536]{2,1,0:T(8,128)(2,1)} %param.18) | copy-start | bytes 294916
  393.3 1.3 copy-start.7
  398.2 9.3 %copy-start.6 = (f32[1,32,8]{1,2,0:T(8,128)S(1)}, f32[1,32,8]{1,2,0:T(8,128)}, u32[]{:S(2)}) copy-start(f32[1,32,8]{1,2,0:T(8,128)} %param.28) | copy-start | bytes 3076
  398.2 86.2 %all-to-all-start.1 = ((bf16[64,1,10,1536]{3,2,1,0:T(8,128)(2,1)}), bf16[64,1,10,1536]{3,2,1,0:T(8,128)(2,1)}, u32[]{:S(2)}, u32[]{:S(2)}) async-start(bf16[64,1,10,1536]{3,2,1,0:T(8,128)(2,1)} %copy.50), calls=%async_computation.2 | async-start | bytes 6291456 | tf_op jit(solution)/shard_map/all_to_all | solution.py:159
Sparse Core Ops, SparseCore 0:
  11.9 135.1 all-gather.1
  242.7 37.1 reduce-scatter.1
where the time goes:
time: 507 us; the launch traced here: 505 us
  waiting for transfers between devices  218 us (43%)
  blocking collectives  112 us (22%)
  local copies, waits for them, and re-layouts  77.9 us (15%)
  loops' own time  44.4 us (9%)
  other arithmetic  16.6 us (3%)
  between operations  13.8 us (3%)
  matrix products  12.2 us (2%)
  starting transfers between devices  9.38 us (2%)
    all_gather x1, waiting for transfers between devices, on_device(): lax.all_gather(prefix_cache, 'req', axis=0, tiled=True)  107 us
    all_to_all x1, blocking collectives, on_device(): lax.all_to_all(outgoing, 'req', split_axis=0, concat_axis=0, tiled=True)  89.7 us
    all_to_all x1, waiting for transfers between devices, on_device(): lax.all_to_all(produced, 'req', split_axis=0, concat_axis=0, tiled=True)  75 us
    another operation x1, loops' own time, on_device(): lax.scan(one_piece, start_state, (lax.all_gather(prefix_cache, 'req', axi...  43.3 us
    dynamic_slice x68, local copies, waits for them, and re-layouts, on_device(): lax.scan(one_piece, start_state, (lax.all_gather(prefix_cache, 'req', axi...  40.8 us
    reduce_scatter x1, waiting for transfers between devices, on_device(): lax.psum_scatter(jnp.dot(mixed, w_out, preferred_element_type=jnp.float32...  35.9 us
    all_gather x1, blocking collectives, on_device(): gathered = lax.all_gather(normed, 'tp', axis=0, tiled=True)  22.7 us
    scatter x2, local copies, waits for them, and re-layouts, on_device(): jnp.zeros((EXPERTS, capacity, D), jnp.bfloat16).at[chosen, slot_in]  20 us
  transfers between devices with their start and end apart: 3, of which 3 were waited for; matrix products, arithmetic and copies ran while one was open for 3% of the time, Pallas kernels for 0%

commit v1 on v0

--- a/solution.py
+++ b/solution.py
@@ -116,7 +116,15 @@
         return (lax.cond(flag, update, lambda inner_state: inner_state, state), None)
 
     result, unused = lax.scan(
-        one_piece, start_state, (lax.all_gather(prefix_cache, "req", axis=0, tiled=True), owned)
+        one_piece,
+        start_state,
+        (
+            jnp.concatenate(
+                lax.all_to_all(jnp.stack([prefix_cache] * lax.axis_size("req")), "req", 0, 0),
+                axis=0,
+            ),
+            owned,
+        ),
     )
     state = result
     key_at = jnp.arange(full_rows)

time: 507 us -> 448 us (0.88)
  waiting for transfers between devices: 218 us -> 111 us
  blocking collectives: 112 us -> 147 us
  starting transfers between devices: 9.38 us -> 29 us
    all_gather x1 -> x0, waiting for transfers between devices: 107 us -> none  [on_device(): lax.all_gather(prefix_cache, 'req', axis=0, tiled=True)]
    all_gather x1, blocking collectives: 22.7 us -> 57.4 us  [on_device(): gathered = lax.all_gather(normed, 'tp', axis=0, tiled=True)]
    all_to_all x0 -> x1, starting transfers between devices: none -> 20 us  [on_device(): lax.all_to_all(jnp.stack([prefix_cache] * lax.axis_size('req')), 'req', 0...]
  transfers between devices with their start and end apart: 3 -> 3, of which waited for: 3 -> 2; matrix products, arithmetic and copies ran while one was open for 3% -> 2% of each run, Pallas kernels for 0% -> 0%
where the time goes in v1:
time: 448 us; the launch traced here: 445 us
  blocking collectives  147 us (33%)
  waiting for transfers between devices  111 us (25%)
  local copies, waits for them, and re-layouts  75.8 us (17%)
  loops' own time  42.6 us (10%)
  starting transfers between devices  29 us (6%)
  other arithmetic  14.1 us (3%)
  between operations  13.9 us (3%)
  matrix products  11.4 us (3%)
    all_to_all x1, blocking collectives, on_device(): lax.all_to_all(outgoing, 'req', split_axis=0, concat_axis=0, tiled=True)  89.7 us
    all_to_all x1, waiting for transfers between devices, on_device(): lax.all_to_all(produced, 'req', split_axis=0, concat_axis=0, tiled=True)  74.4 us
    all_gather x1, blocking collectives, on_device(): gathered = lax.all_gather(normed, 'tp', axis=0, tiled=True)  57.4 us
    another operation x1, loops' own time, on_device(): lax.scan(one_piece, start_state, (jnp.concatenate(lax.all_to_all(jnp.stac...  41.4 us
    dynamic_slice x68, local copies, waits for them, and re-layouts, on_device(): lax.scan(one_piece, start_state, (jnp.concatenate(lax.all_to_all(jnp.stac...  41.3 us
    reduce_scatter x1, waiting for transfers between devices, on_device(): lax.psum_scatter(jnp.dot(mixed, w_out, preferred_element_type=jnp.float32...  36.5 us
    scatter x2, local copies, waits for them, and re-layouts, on_device(): jnp.zeros((EXPERTS, capacity, D), jnp.bfloat16).at[chosen, slot_in]  20 us
    all_to_all x1, starting transfers between devices, on_device(): lax.all_to_all(jnp.stack([prefix_cache] * lax.axis_size('req')), 'req', 0...  20 us
  transfers between devices with their start and end apart: 3, of which 2 were waited for; matrix products, arithmetic and copies ran while one was open for 2% of the time, Pallas kernels for 0%

profile of v1, /device:TPU:1, one launch (start us, length us, event | category | flops | bytes accessed | tf_op | source)
XLA Modules:
  0.0 444.7 jit_solution(1493313338891734780)
XLA Ops:
  7.5 1.8 stack.2
  9.3 20.0 %all-to-all-start = ((bf16[64,1,128,128]{2,3,1,0:T(8,128)(2,1)}), bf16[64,1,128,128]{2,3,1,0:T(8,128)(2,1)}, u32[]{:S(2)}, u32[]{:S(2)}) async-start(bf16[64,1,128,128]{2,3,1,0:T(8,128)(2,1)} %stack.2), calls=%async_computation | async-start | bytes 4194304 | tf_op jit(solution)/shard_map/all_to_all | solution.py:123
  29.9 57.4 %all_gather.3 = bf16[256,1536]{1,0:T(8,128)(2,1)S(1)} all-gather(bf16[32,1536]{1,0:T(8,128)(2,1)S(1)} %fusion.37), channel_id=1, replica_groups=mesh['req'=64,'tp'=8] {'tp'}, dimensions={0}, use_global_device_ids=true | all-gather | bytes 884736 | tf_op jit(solution)/shard_map/all_gather | solution.py:80
  90.9 1.4 fusion.80
  93.4 86.2 %while.14 = (s32[]{:T(128)}, f32[1,768]{1,0:T(1,128)S(1)}, f32[1,768]{1,0:T(1,128)S(1)}, f32[1,768,64]{1,2,0:T(8,128)S(1)}, pred[64]{0:T(512)(128)(4,1)S(1)}, /*...) while((s32[]{:T(128)}, f32[1,768]{1,0:T(1,128)S(1)}, f32[1,768]{1,0:T(1,128)S(1)}, ...), condition=%wide.region_7.8_spmd, body=%wide.region_2.7_spmd.sunk | while | flops 25856260 | bytes 1922252 | solution.py:118
  100.9 1.4 conditional.2
  132.6 1.4 conditional.2
  140.3 1.4 conditional.2
  156.8 1.4 conditional.2
  181.3 1.3 convolution_convert_fusion.1
  183.9 36.5 %reduce-scatter.2.cloned.1.call-done = bf16[32,1536]{1,0:T(8,128)(2,1)} async-done(((bf16[256,1536]{1,0:T(8,128)(2,1)}), bf16[32,1536]{1,0:T(8,128)(2,1)}) %reduce-scatter.2.cloned.1.call-update) | async-done | bytes 98320 | tf_op jit(solution)/shard_map/reduce_scatter | solution.py:138
  222.5 1.3 gather_fusion
  223.8 19.5 %scatter_fusion = bf16[32,10,1536]{2,0,1:T(8,128)(2,1)S(1)} fusion(bf16[32,10,1536]{2,0,1:T(8,128)(2,1)S(1)} %broadcast_in_dim.99, s32[256]{0:T(256)S(1)} %bitcast.145, bf16[256,1536]{1,0:T(8,128)(2,1)S(1)} %gather_fusion), kind=kCustom, calls=%fused_computation.2 | custom fusion | bytes 2361344 | tf_op jit(solution)/shard_map/scatter | solution.py:152
  244.2 89.7 %all_to_all.15 = bf16[64,1,10,1536]{3,2,1,0:T(8,128)(2,1)S(1)} all-to-all(bf16[64,1,10,1536]{3,2,1,0:T(8,128)(2,1)S(1)} %bitcast.146), channel_id=1, replica_groups=mesh['req'=64,'tp'=8] {'req'}, dimensions={0} | all-to-all | bytes 3932160 | tf_op jit(solution)/shard_map/all_to_all | solution.py:159
  333.9 1.3 fusion.14
  335.9 2.9 copy.50
  338.8 9.0 %all-to-all-start.2 = ((bf16[64,1,10,1536]{3,2,1,0:T(8,128)(2,1)}), bf16[64,1,10,1536]{3,2,1,0:T(8,128)(2,1)}, u32[]{:S(2)}, u32[]{:S(2)}) async-start(bf16[64,1,10,1536]{3,2,1,0:T(8,128)(2,1)} %copy.50), calls=%async_computation.3 | async-start | bytes 6291456 | tf_op jit(solution)/shard_map/all_to_all | solution.py:167
  347.9 1.2 add_compare_fusion
  349.7 74.4 %all-to-all-done.2 = bf16[64,1,10,1536]{3,2,1,0:T(8,128)(2,1)} async-done(((bf16[64,1,10,1536]{3,2,1,0:T(8,128)(2,1)}), bf16[64,1,10,1536]{3,2,1,0:T(8,128)(2,1)}, u32[]{:S(2)}, u32[]{:S(2)}) %all-to-all-start.2) | async-done | bytes 1966112 | tf_op jit(solution)/shard_map/all_to_all | solution.py:167
  424.1 4.8 %convert_reduce_fusion = f32[32,10,1536]{2,1,0:T(8,128)} fusion(bf16[32,2,10,1536]{3,2,1,0:T(8,128)(2,1)} %bitcast.142), kind=kLoop, calls=%fused_computation.18 | loop fusion | flops 1474560 | bytes 3932160 | tf_op jit(solution)/shard_map/reduce_sum | solution.py:168
  428.9 2.0 reshape.453
  430.9 2.5 gather_fusion.1
  433.4 2.8 fusion.11
  436.2 1.7 fusion.44
  (237 shorter events, 58.0 us)
Async XLA Ops:
  6.5 327.4 %copy-start = (bf16[1,1536,512]{2,1,0:T(8,128)(2,1)S(1)}, bf16[1,1536,512]{2,1,0:T(8,128)(2,1)}, u32[]{:S(2)}) copy-start(bf16[1,1536,512]{2,1,0:T(8,128)(2,1)} %param.25) | copy-start | bytes 4718596
  9.3 20.1 %copy-start.5 = (bf16[1536]{0:T(1024)(128)(2,1)S(1)}, bf16[1536]{0:T(1024)(128)(2,1)}, u32[]{:S(2)}) copy-start(bf16[1536]{0:T(1024)(128)(2,1)} %param.19) | copy-start | bytes 9220
  9.3 20.1 %copy-start.1 = (bf16[1,32,1536]{2,1,0:T(8,128)(2,1)S(1)}, bf16[1,32,1536]{2,1,0:T(8,128)(2,1)}, u32[]{:S(2)}) copy-start(bf16[1,32,1536]{2,1,0:T(8,128)(2,1)} %param.18) | copy-start | bytes 294916
  9.3 78.0 %copy-start.2 = (bf16[1536,192]{0,1:T(8,128)(2,1)S(1)}, bf16[1536,192]{0,1:T(8,128)(2,1)}, u32[]{:S(2)}) copy-start(bf16[1536,192]{0,1:T(8,128)(2,1)} %param.21) | copy-start | bytes 1769476
  9.3 84.0 %all-to-all-start = ((bf16[64,1,128,128]{2,3,1,0:T(8,128)(2,1)}), bf16[64,1,128,128]{2,3,1,0:T(8,128)(2,1)}, u32[]{:S(2)}, u32[]{:S(2)}) async-start(bf16[64,1,128,128]{2,3,1,0:T(8,128)(2,1)} %stack.2), calls=%async_computation | async-start | bytes 4194304 | tf_op jit(solution)/shard_map/all_to_all | solution.py:123
  29.3 191.1 %reduce-scatter.2.cloned.1.call-start = ((), (), s32[]{:S(2)}) async-start(), calls=%async_computation.4 | async-start | bytes 884736 | tf_op jit(solution)/shard_map/reduce_scatter | solution.py:138
  29.9 58.4 %copy-start.10 = (s32[64]{0:T(128)S(1)}, s32[64]{0:T(128)}, u32[]{:S(2)}) copy-start(s32[64]{0:T(128)} %param.29) | copy-start | bytes 772
  29.9 59.0 %copy-start.11 = (s32[64]{0:T(128)S(1)}, s32[64]{0:T(128)}, u32[]{:S(2)}) copy-start(s32[64]{0:T(128)} %param.30) | copy-start | bytes 772
  29.9 60.2 %copy-start.12 = (s32[64]{0:T(128)S(1)}, s32[64]{0:T(128)}, u32[]{:S(2)}) copy-start(s32[64]{0:T(128)} %param.31) | copy-start | bytes 772
  92.3 0.6 copy-start.4
  179.6 1.6 copy-start.3
  180.0 2.6 copy-start.6
  180.0 3.0 copy-start.7
  333.9 1.3 copy-start.9
  338.8 9.0 %copy-start.8 = (f32[1,32,8]{1,2,0:T(8,128)S(1)}, f32[1,32,8]{1,2,0:T(8,128)}, u32[]{:S(2)}) copy-start(f32[1,32,8]{1,2,0:T(8,128)} %param.28) | copy-start | bytes 3076
  338.8 85.3 %all-to-all-start.2 = ((bf16[64,1,10,1536]{3,2,1,0:T(8,128)(2,1)}), bf16[64,1,10,1536]{3,2,1,0:T(8,128)(2,1)}, u32[]{:S(2)}, u32[]{:S(2)}) async-start(bf16[64,1,10,1536]{3,2,1,0:T(8,128)(2,1)} %copy.50), calls=%async_computation.3 | async-start | bytes 6291456 | tf_op jit(solution)/shard_map/all_to_all | solution.py:167
Sparse Core Ops, SparseCore 0:
  182.7 37.6 reduce-scatter.1
